TPU v7x, 32 devices: a whole 2x2x4 slice. The times are simulated.
32 devices in a mesh: seq: 16 (over z, y, x), head: 2 (over core).
Axes of the slice: x: 2, y: 2, z: 4, core: 2. Of those that a mesh axis runs over, the one named last changes fastest.
Arguments:
- queries: bfloat16 [6144, 2048], P('seq', 'head'), may hold values from -6 to 6
- keys: bfloat16 [6144, 2048], P('seq', 'head'), may hold values from -0.5 to 0.5
- values: bfloat16 [6144, 2048], P('seq', 'head'), may hold values from -6 to 6
- level_pattern: int32 [6144], P('seq'), may hold values from 0 to 15
- level_weight: float32 [16, 9], replicated, may hold values from 0.5 to 2
- out_weight: bfloat16 [2, 1024, 2048], P('head', 'seq'), may hold values from -0.125 to 0.125
Outputs:
- mixed: float32 [6144, 2048], P('seq', 'head')
All inputs are finite; a program needn't handle non-finite values.
Results may differ from a plain program's by a relative error of at most 0.003.
Values may be sent and summed in bfloat16 or wider, within the bound.
A program may use at most 64 MiB of HBM per device.

v0:
```python
import math

import jax
import jax.numpy as jnp
from jax import lax
from jax.sharding import PartitionSpec as P

HD = 128


def swapped(x, axis, stride):
    return lax.ppermute(x, axis, [(i, i ^ 1 << stride) for i in range(lax.axis_size(axis))])


def on_device(queries, keys, values, level_pattern, level_weight, out_weight):
    highest = lax.Precision.HIGHEST
    tokens_here = queries.shape[0]
    head_count = queries.shape[1] // HD
    query = queries.reshape(tokens_here, head_count, HD)
    key_mat = keys.reshape(tokens_here, head_count, HD)
    value_mat = values.reshape(tokens_here, head_count, HD)
    scores = jnp.einsum("the,she->hts", query, key_mat, preferred_element_type=jnp.float32)
    row_pos = lax.broadcasted_iota(jnp.int32, (tokens_here, tokens_here), 0)
    col_pos = lax.broadcasted_iota(jnp.int32, (tokens_here, tokens_here), 1)
    inner = jnp.where((col_pos <= row_pos)[None], scores, 0.0).astype(jnp.bfloat16)
    within = jnp.einsum("hts,shf->thf", inner, value_mat, preferred_element_type=jnp.float32)
    within = within * (1.0 / math.sqrt(tokens_here))
    pattern_ids = lax.broadcasted_iota(jnp.int32, (tokens_here, level_weight.shape[0]), 1)
    one_hot = (level_pattern[:, None] == pattern_ids).astype(jnp.float32)
    level_mix = jnp.dot(
        one_hot, level_weight, precision=highest, preferred_element_type=jnp.float32
    )
    states = jnp.einsum("she,shf->hef", key_mat, value_mat, preferred_element_type=jnp.float32)
    position = lax.axis_index("seq")
    bit_count = lax.axis_size("seq").bit_length() - 1
    subtree = states
    blocks = []
    level_coef = []
    for bit_index in range(bit_count):
        sibling = swapped(subtree, "seq", bit_index)
        active = (position // 2**bit_index % 2).astype(jnp.float32)
        factor = 1.0 / math.sqrt(2**bit_index * tokens_here)
        blocks.append(sibling)
        level_coef.append(level_mix[:, bit_index + 1] * active * factor)
        subtree = subtree + sibling
    level_reads = jnp.einsum(
        "the,lhef->lthf", query.astype(jnp.float32), jnp.stack(blocks), precision=highest
    )
    combined = jnp.einsum("lthf,lt->thf", level_reads, jnp.stack(level_coef), precision=highest)
    attended = level_mix[:, 0, None, None] * within + combined
    attended = attended.reshape(tokens_here, head_count * HD).astype(jnp.bfloat16)
    partial_value = jnp.dot(
        attended,
        lax.all_gather(out_weight, "seq", axis=1, tiled=True)[0],
        preferred_element_type=jnp.float32,
    )
    mixed = lax.psum_scatter(partial_value, "head", scatter_dimension=1, tiled=True)
    return mixed


def solution(mesh):
    placed = (
        P("seq", "head"),
        P("seq", "head"),
        P("seq", "head"),
        P("seq"),
        P(),
        P("head", "seq", None),
    )
    return jax.shard_map(
        on_device, mesh=mesh, in_specs=placed, out_specs=P("seq", "head"), check_vma=False
    )
```

profile of v0, /device:TPU:28, one launch (start us, length us, event | category | flops | bytes accessed | tf_op | source)
XLA Modules:
  0.0 136.2 jit_solution(16479728716966614512)
XLA Ops:
  6.5 0.0 copy-start
  6.5 0.0 all-gather.2.cloned.1.call-start
  6.5 0.7 all-gather.2.cloned.1.call-update
  7.3 0.0 reduce-scatter.2.cloned.1.call-start
  7.3 1.5 %copy.19 = bf16[384,1024]{0,1:T(8,128)(2,1)S(1)} copy(bf16[384,1024]{1,0:T(8,128)(2,1)} %param.7) | data formatting | bytes 1572864 | tf_op jit(solution)/shard_map/reshape | solution.py:20
  8.8 0.0 copy-done
  8.8 0.4 fusion.11
  9.2 0.0 copy-start.5
  9.2 0.0 copy-start.6
  9.2 0.0 copy-start.1
  9.2 1.6 %collective-permute-start = (f32[8,128,128]{2,1,0:T(8,128)S(1)}, f32[8,128,128]{2,1,0:T(8,128)S(1)}, u32[]{:S(2)}, u32[]{:S(2)}) collective-permute-start(f32[8,128,128]{2,1,0:T(8,128)S(1)} %fusion.11), channel_id=1, source_target_pairs={{0,2},{2,0},{4,6},{6,4},{8,10},{10,8},{12,14},{14,12},{16,18},{18,... | collective-permute-start | bytes 1572872 | tf_op jit(solution)/shard_map/ppermute | solution.py:12
  10.8 13.5 %collective-permute-done = f32[8,128,128]{2,1,0:T(8,128)S(1)} collective-permute-done((f32[8,128,128]{2,1,0:T(8,128)S(1)}, f32[8,128,128]{2,1,0:T(8,128)S(1)}, u32[]{:S(2)}, u32[]{:S(2)}) %collective-permute-start) | collective-permute-done | bytes 524320 | tf_op jit(solution)/shard_map/ppermute | solution.py:12
  24.2 0.0 copy-start.2
  24.2 0.1 add.31
  24.3 0.5 collective-permute-start.1
  24.8 0.2 copy-done.2
  25.0 10.9 %collective-permute-done.1 = f32[8,128,128]{2,1,0:T(8,128)S(1)} collective-permute-done((f32[8,128,128]{2,1,0:T(8,128)S(1)}, f32[8,128,128]{2,1,0:T(8,128)S(1)}, u32[]{:S(2)}, u32[]{:S(2)}) %collective-permute-start.1) | collective-permute-done | bytes 524320 | tf_op jit(solution)/shard_map/ppermute | solution.py:12
  35.9 0.0 copy-start.3
  35.9 0.1 add.32
  36.0 0.6 collective-permute-start.2
  36.6 23.4 %collective-permute-done.2 = f32[8,128,128]{2,1,0:T(8,128)S(1)} collective-permute-done((f32[8,128,128]{2,1,0:T(8,128)S(1)}, f32[8,128,128]{2,1,0:T(8,128)S(1)}, u32[]{:S(2)}, u32[]{:S(2)}) %collective-permute-start.2) | collective-permute-done | bytes 524320 | tf_op jit(solution)/shard_map/ppermute | solution.py:12
  60.0 0.0 copy-start.4
  60.0 0.9 add.33
  60.9 0.0 copy-done.3
  60.9 0.3 collective-permute-start.3
  61.2 0.0 copy-done.4
  61.2 0.0 copy-done.5
  61.2 0.0 copy-done.6
  61.2 0.3 fusion.19
  61.5 0.0 copy-done.1
  61.5 0.4 copy.20
  62.0 39.3 %collective-permute-done.3 = f32[8,128,128]{2,1,0:T(8,128)} collective-permute-done((f32[8,128,128]{2,1,0:T(8,128)}, f32[8,128,128]{2,1,0:T(8,128)}, u32[]{:S(2)}, u32[]{:S(2)}) %collective-permute-start.3) | collective-permute-done | bytes 524320 | tf_op jit(solution)/shard_map/ppermute | solution.py:12
  101.3 5.7 %fusion = f32[384,8,128]{0,2,1:T(8,128)} fusion(f32[384,4]{0,1:T(4,128)S(1)} %maximum_bitcast_fusion, bf16[384,8,128,1]{0,2,3,1:T(8,128)(2,1)S(1)} %bitcast.59, f32[1,8,128,128]{3,2,1,0:T(8,128)} %bitcast.7, f32[1,8,128,128]{3,2,1,0:T(8,128)} %bitcast.62, f32[1,8,128,128]{3,2,1,0:T(8,128)} %bitcast.61, f32[1,8,128,128]{3,2,1,0:T(8,128)} %bitcast.60), kind=kOutput, calls=%fused_computation.1 | convolution fusion | flops 2420244480 | bytes 4462592 | tf_op jit(solution)/shard_map/the,lhef->lthf/dot_general | solution.py:46
  107.0 2.9 %fusion.9 = bf16[384,8,128]{0,2,1:T(8,128)(2,1)S(1)} fusion(f32[384,8,128]{0,2,1:T(8,128)} %fusion, pred[384,384]{1,0:T(8,128)(4,1)S(1)} %iota_compare_fusion, bf16[384,8,128]{0,2,1:T(8,128)(2,1)S(1)} %bitcast.57, f32[384]{0:T(512)S(1)} %get-tuple-element.5, bf16[384,1024]{1,0:T(8,128)(2,1)S(1)} %copy-done, bf16[384,1024]{1,0:T(8,128)(2,1)S(1)} %copy-done.1), kind=kOutput, calls=%fused_computation.12 | convolution fusion | flops 607518720 | bytes 4867584 | tf_op jit(solution)/shard_map/hts,shf->thf/dot_general | solution.py:26
  109.9 0.0 all-gather.2.cloned.1.call-done
  109.9 5.7 %fusion.1 = f32[384,2048]{1,0:T(8,128)} fusion(bf16[384,1024]{0,1:T(8,128)(2,1)S(1)} %bitcast.58, bf16[1,1024,2048]{2,1,0:T(8,128)(2,1)} %all-gather.2.cloned.1.call-done), kind=kOutput, calls=%fused_computation.3 | convolution fusion | flops 1610612736 | bytes 8126464 | tf_op jit(solution)/shard_map/dot_general | solution.py:52
  115.6 0.0 reduce-scatter.2.cloned.1.call-update
  115.6 13.8 %reduce-scatter.2.cloned.1.call-done = f32[384,1024]{1,0:T(8,128)} async-done(((f32[384,2048]{1,0:T(8,128)}), f32[384,1024]{1,0:T(8,128)}) %reduce-scatter.2.cloned.1.call-update) | async-done | bytes 1572880 | tf_op jit(solution)/shard_map/reduce_scatter | solution.py:57
  (3 shorter events, 0.1 us)
Async XLA Ops:
  6.5 2.3 %copy-start = (bf16[384,1024]{1,0:T(8,128)(2,1)S(1)}, bf16[384,1024]{1,0:T(8,128)(2,1)}, u32[]{:S(2)}) copy-start(bf16[384,1024]{1,0:T(8,128)(2,1)} %param.8) | copy-start | bytes 2359300
  6.5 103.4 %all-gather.2.cloned.1.call-start = ((), (), s32[]{:S(2)}) async-start(), calls=%async_computation.1 | async-start | bytes 4456448 | tf_op jit(solution)/shard_map/all_gather | solution.py:54
  7.3 122.1 %reduce-scatter.2.cloned.1.call-start = ((), (), s32[]{:S(2)}) async-start(), calls=%async_computation.2 | async-start | bytes 4718592 | tf_op jit(solution)/shard_map/reduce_scatter | solution.py:57
  9.2 52.0 %copy-start.5 = (f32[16,9]{1,0:T(8,128)S(1)}, f32[16,9]{1,0:T(8,128)}, u32[]{:S(2)}) copy-start(f32[16,9]{1,0:T(8,128)} %param.10) | copy-start | bytes 1732
  9.2 52.0 %copy-start.6 = (s32[384]{0:T(512)S(1)}, s32[384]{0:T(512)}, u32[]{:S(2)}) copy-start(s32[384]{0:T(512)} %param.9) | copy-start | bytes 4612
  9.2 52.3 %copy-start.1 = (bf16[384,1024]{1,0:T(8,128)(2,1)S(1)}, bf16[384,1024]{1,0:T(8,128)(2,1)}, u32[]{:S(2)}) copy-start(bf16[384,1024]{1,0:T(8,128)(2,1)} %param.6) | copy-start | bytes 2359300
  9.2 15.0 %collective-permute-start = (f32[8,128,128]{2,1,0:T(8,128)S(1)}, f32[8,128,128]{2,1,0:T(8,128)S(1)}, u32[]{:S(2)}, u32[]{:S(2)}) collective-permute-start(f32[8,128,128]{2,1,0:T(8,128)S(1)} %fusion.11), channel_id=1, source_target_pairs={{0,2},{2,0},{4,6},{6,4},{8,10},{10,8},{12,14},{14,12},{16,18},{18,... | collective-permute-start | bytes 1572872 | tf_op jit(solution)/shard_map/ppermute | solution.py:12
  24.2 0.8 copy-start.2
  24.3 11.6 %collective-permute-start.1 = (f32[8,128,128]{2,1,0:T(8,128)S(1)}, f32[8,128,128]{2,1,0:T(8,128)S(1)}, u32[]{:S(2)}, u32[]{:S(2)}) collective-permute-start(f32[8,128,128]{2,1,0:T(8,128)S(1)} %add.31), channel_id=1, source_target_pairs={{0,4},{2,6},{4,0},{6,2},{8,12},{10,14},{12,8},{14,10},{16,20},{18,... | collective-permute-start | bytes 1572872 | tf_op jit(solution)/shard_map/ppermute | solution.py:12
  35.9 25.0 %copy-start.3 = (f32[8,128,128]{2,1,0:T(8,128)}, f32[8,128,128]{2,1,0:T(8,128)S(1)}, u32[]{:S(2)}) copy-start(f32[8,128,128]{2,1,0:T(8,128)S(1)} %collective-permute-done.1) | copy-start | bytes 1572868
  36.0 24.0 %collective-permute-start.2 = (f32[8,128,128]{2,1,0:T(8,128)S(1)}, f32[8,128,128]{2,1,0:T(8,128)S(1)}, u32[]{:S(2)}, u32[]{:S(2)}) collective-permute-start(f32[8,128,128]{2,1,0:T(8,128)S(1)} %add.32), channel_id=1, source_target_pairs={{0,8},{2,10},{4,12},{6,14},{8,0},{10,2},{12,4},{14,6},{16,24},{18,... | collective-permute-start | bytes 1572872 | tf_op jit(solution)/shard_map/ppermute | solution.py:12
  60.0 1.2 copy-start.4
  60.9 40.4 %collective-permute-start.3 = (f32[8,128,128]{2,1,0:T(8,128)}, f32[8,128,128]{2,1,0:T(8,128)}, u32[]{:S(2)}, u32[]{:S(2)}) collective-permute-start(f32[8,128,128]{2,1,0:T(8,128)} %add.33), channel_id=1, source_target_pairs={{0,16},{2,18},{4,20},{6,22},{8,24},{10,26},{12,28},{14,30},{16,0},... | collective-permute-start | bytes 1572872 | tf_op jit(solution)/shard_map/ppermute | solution.py:12
Sparse Core Ops, SparseCore 0:
  10.1 91.7 all-gather.1
  115.7 13.6 reduce-scatter.1
where the time goes:
time: 138 us; the launch traced here: 136 us
  waiting for transfers between devices  102 us (74%)
  matrix products  14.9 us (11%)
  between operations  13.5 us (10%)
  starting transfers between devices  2.96 us (2%)
  local copies, waits for them, and re-layouts  2.08 us (2%)
    ppermute x4, waiting for transfers between devices, swapped(): lax.ppermute(x, axis, [(i, i ^ 1 << stride) for i in range(lax.axis_size(...  87.1 us
    reduce_scatter x1, waiting for transfers between devices, on_device(): lax.psum_scatter(partial_value, 'head', scatter_dimension=1, tiled=True)  13.8 us
    dot_general x1, matrix products, on_device(): jnp.einsum('the,lhef->lthf', query.astype(jnp.float32), jnp.stack(blocks)...  5.73 us
    dot_general x1, matrix products, on_device(): jnp.dot(attended, lax.all_gather(out_weight, 'seq', axis=1, tiled=True)[0...  5.69 us
    ppermute x4, starting transfers between devices, swapped(): lax.ppermute(x, axis, [(i, i ^ 1 << stride) for i in range(lax.axis_size(...  2.92 us
    dot_general x1, matrix products, on_device(): jnp.einsum('hts,shf->thf', inner, value_mat, preferred_element_type=jnp.f...  2.86 us
  transfers between devices with their start and end apart: 6, of which 5 were waited for; matrix products, arithmetic and copies ran while one was open for 9% of the time, Pallas kernels for 0%

commit v1 on v0

v1 whole, which is shorter than its diff:
```python
import functools
import itertools
import math

import jax
import jax.numpy as jnp
from jax import lax
from jax.experimental import pallas as pl
from jax.experimental.pallas import tpu as pltpu
from jax.sharding import PartitionSpec as P

HD = 128
MESH = pl.DeviceIdType.MESH


def line_dims(mesh):
    n = mesh.shape["seq"]
    devices = mesh.devices.reshape(n, -1)[:, 0]
    coords = [tuple(getattr(d, "coords", ())) for d in devices]
    dims = []
    if len(set(coords)) == n:
        for axis in range(len(coords[0])):
            seen = [c[axis] - coords[0][axis] for c in coords]
            length = max(seen) + 1
            if length > 1:
                dims.append((length, seen.index(1)))
    stride = 1
    for length, step in sorted(dims, key=lambda d: d[1]):
        if step != stride:
            break
        stride *= length
    if not dims or stride != n:
        dims = [(2, 1 << i) for i in range(n.bit_length() - 1)]
    return sorted(dims, key=lambda d: -d[1])


def nearest(k, p, n):
    m = jnp.minimum(p, n - 1 - p)
    sign = jnp.where(p == m, 1, -1)
    near = (k + 1) // 2 * (2 * (k % 2) - 1)
    if n == 2:
        return p + k * (1 - 2 * p)
    return jnp.where(k <= 2 * m, p + near, p + sign * (k - m))


def kernel(
    plan, q_hbm, k_hbm, v_hbm, pattern_ref, table_ref, w_hbm, *rest
):
    dims, orders, cuts, events, n, fused = plan
    if fused:
        out_ref, *rest = rest
    else:
        att_hbm, w_out_hbm, *rest = rest
    (q_ref, k_ref, v_ref, w_ref, wbuf, att, acc, sub, outgoing, incoming, mixb,
     load_sem, own_sem, pair_send, pair_recv, w_send, w_recv, s_send, s_recv, a_send, a_recv) = rest
    me = lax.axis_index("seq")
    core = lax.axis_index("head")
    other = 1 - core
    tokens, width = q_ref.shape
    heads = width // HD
    cols = wbuf.shape[-1]
    bits = n.bit_length() - 1
    groups = a_send.shape[0]
    per = heads // groups
    place = [me // stride % length for length, stride in dims]

    loads = [
        pltpu.make_async_copy(src, dst, load_sem.at[i])
        for i, (src, dst) in enumerate(((w_hbm, w_ref), (k_hbm, k_ref), (v_hbm, v_ref), (q_hbm, q_ref)))
    ]
    for load in loads:
        load.start()

    barrier = pltpu.get_barrier_semaphore()
    total = 1
    pl.semaphore_signal(barrier, inc=1, device_id=(me, other), device_id_type=MESH)
    for bit in range(bits):
        pl.semaphore_signal(barrier, inc=1, device_id=(me ^ (1 << bit), core), device_id_type=MESH)
        total += 1
    for (length, stride), p in zip(dims, place):
        if length == 2:
            continue
        for step in (-1, 1):
            there = jnp.logical_and(p + step >= 0, p + step < length)

            @pl.when(there)
            def _():
                pl.semaphore_signal(barrier, inc=1, device_id=(me + step * stride, core), device_id_type=MESH)

            total = total + there.astype(jnp.int32)

    for l in range(bits + 1):
        if l == 0:
            ids = lax.broadcasted_iota(jnp.int32, (table_ref.shape[0], tokens), 0)
            one_hot = (ids == pattern_ref[...]).astype(jnp.float32)
            mix = lax.dot_general(
                one_hot, table_ref[...], (((0,), (0,)), ((), ())),
                precision=lax.Precision.HIGHEST, preferred_element_type=jnp.float32,
            )
        factor = 1.0 / math.sqrt(tokens * (1 if l == 0 else 2 ** (l - 1)))
        mixb[l] = jnp.broadcast_to(mix[:, l : l + 1] * factor, (tokens, HD))

    def head_cols(h):
        return slice(h * HD, (h + 1) * HD)

    loads[1].wait()
    loads[2].wait()

    def make_states(h):
        state = lax.dot_general(
            k_ref[:, head_cols(h)], v_ref[:, head_cols(h)], (((0,), (0,)), ((), ())),
            preferred_element_type=jnp.float32,
        )
        sub[h] = state
        outgoing[0, h] = state.astype(jnp.bfloat16)

    for h in range(heads):
        make_states(h)
    loads[0].wait()
    pl.semaphore_wait(barrier, total)

    def pair_copy():
        return pltpu.make_async_remote_copy(
            src_ref=w_ref.at[0, :, pl.ds(pl.multiple_of(other * cols, 128), cols)],
            dst_ref=wbuf.at[core, me], send_sem=pair_send, recv_sem=pair_recv,
            device_id=(me, other), device_id_type=MESH,
        )

    def pair_landed():
        return pltpu.make_async_remote_copy(
            src_ref=w_ref.at[0, :, pl.ds(pl.multiple_of(other * cols, 128), cols)],
            dst_ref=wbuf.at[other, me], send_sem=pair_send, recv_sem=pair_recv,
            device_id=(me, other), device_id_type=MESH,
        )

    pair_copy().start()
    own = pltpu.make_async_copy(
        w_ref.at[0, :, pl.ds(pl.multiple_of(core * cols, 128), cols)], wbuf.at[core, me], own_sem
    )
    own.start()

    def state_copy(level, group):
        piece = pl.ds(group * per, per)
        return pltpu.make_async_remote_copy(
            src_ref=outgoing.at[level, piece], dst_ref=incoming.at[level, piece],
            send_sem=s_send.at[level, group], recv_sem=s_recv.at[level, group],
            device_id=(me ^ (1 << level), core), device_id_type=MESH,
        )

    def sum_needed(level):
        return me // 2 ** (level + 1) != n // 2 ** (level + 1) - 1

    def active(level):
        return me // 2**level % 2 == 1

    def sends(level):
        return jnp.logical_or(jnp.logical_not(active(level)), sum_needed(level))

    def receives(level):
        return jnp.logical_or(active(level), sum_needed(level))

    for group in range(groups):
        @pl.when(sends(0))
        def _():
            state_copy(0, group).start()

    def weight_copy(part, source, slot, target):
        lo, size = cuts[part]
        piece = wbuf.at[:, source, :, pl.ds(lo, size)]
        return pltpu.make_async_remote_copy(
            src_ref=piece, dst_ref=piece,
            send_sem=w_send.at[part, source if fused else 0, slot], recv_sem=w_recv.at[part, source],
            device_id=(target, core), device_id_type=MESH,
        )

    def forward(part, source, at, arrived, action):
        order = orders[part]
        for rank in range(max(arrived, 0), len(order)):
            d = order[rank]
            length, stride = dims[d]
            for slot, step in ((2 * rank, 1), (2 * rank + 1, -1)):
                if rank == arrived and length == 2:
                    continue
                ok = jnp.logical_and(place[d] + step >= 0, place[d] + step < length)
                if rank == arrived:
                    ok = jnp.logical_and(ok, (place[d] - at[d]) * step > 0)

                @pl.when(ok)
                def _():
                    copy = weight_copy(part, source, slot, me + step * stride)
                    if action == "start":
                        copy.start()
                    else:
                        copy.wait_send()

    def source_of(part, ks):
        at = {d: nearest(k, place[d], dims[d][0]) for d, k in zip(orders[part], ks)}
        return at, sum(at[d] * dims[d][1] for d in at)

    def arrived_by(ks):
        return max((r for r, k in enumerate(ks) if k), default=-1)

    def weight_event(part, ks, arrived):
        at, source = source_of(part, ks)
        weight_copy(part, source, 0, me).wait_recv()
        forward(part, source, at, arrived, "start")
        if not fused:
            forward(part, source, at, arrived, "wait")

    def read_state(level, h):
        acc[:, head_cols(h)] += mixb[level + 1] * jnp.dot(
            q_ref[:, head_cols(h)], incoming[level, h], preferred_element_type=jnp.float32
        )

    def within_event(h):
        columns = head_cols(h)
        scores = lax.dot_general(
            q_ref[:, columns], k_ref[:, columns], (((1,), (1,)), ((), ())),
            preferred_element_type=jnp.float32,
        )
        row = lax.broadcasted_iota(jnp.int32, (tokens, tokens), 0)
        col = lax.broadcasted_iota(jnp.int32, (tokens, tokens), 1)
        inner = jnp.where(col <= row, scores, 0.0).astype(jnp.bfloat16)
        acc[:, columns] = mixb[0] * jnp.dot(inner, v_ref[:, columns], preferred_element_type=jnp.float32)

    def att_copy(group, mine):
        columns = pl.ds(group * per * HD, per * HD)
        which = core if mine else other
        return pltpu.make_async_remote_copy(
            src_ref=att.at[core, :, columns], dst_ref=att.at[which, :, columns],
            send_sem=a_send.at[group], recv_sem=a_recv.at[group],
            device_id=(me, other), device_id_type=MESH,
        )

    def state_event(level, group):
        @pl.when(receives(level))
        def _():
            state_copy(level, group).wait_recv()

        span = range(group * per, (group + 1) * per)
        if level + 1 < bits:
            @pl.when(sum_needed(level))
            def _():
                for h in span:
                    summed = sub[h] + incoming[level, h].astype(jnp.float32)
                    sub[h] = summed
                    outgoing[level + 1, h] = summed.astype(jnp.bfloat16)

            @pl.when(sends(level + 1))
            def _():
                state_copy(level + 1, group).start()

        @pl.when(active(level))
        def _():
            for h in span:
                read_state(level, h)

        if level + 1 == bits:
            columns = slice(group * per * HD, (group + 1) * per * HD)
            att[core, :, columns] = acc[:, columns].astype(jnp.bfloat16)
            att_copy(group, True).start()

    own.wait()
    pair_landed().wait_recv()
    for part in range(len(orders)):
        at, source = source_of(part, (0,) * len(dims))
        forward(part, source, at, -1, "start")
        if not fused:
            forward(part, source, at, -1, "wait")
    loads[3].wait()

    def project(part):
        lo, size = cuts[part]
        columns = slice(lo, lo + size)
        flat = [wbuf[g, :, :, columns].reshape(-1, size) for g in range(2)]
        out_ref[:, columns] = jnp.dot(att[0], flat[0], preferred_element_type=jnp.float32) + jnp.dot(
            att[1], flat[1], preferred_element_type=jnp.float32
        )

    for event in events:
        if event[0] == "within":
            within_event(event[1])
        elif event[0] == "state":
            state_event(event[1], event[2])
        elif event[0] == "weight":
            weight_event(*event[1:])
        elif event[0] == "loop":
            lengths = [[dims[d][0] for d in order] for order in orders]

            def each(e, carry):
                for part, order in enumerate(orders):
                    for arrived in range(len(order)):
                        below = math.prod(lengths[part][:arrived])
                        ks = []
                        rest_e = e
                        for length in lengths[part]:
                            ks.append(rest_e % length)
                            rest_e = rest_e // length

                        @pl.when(jnp.logical_and(e >= below, e < below * lengths[part][arrived]))
                        def _():
                            weight_event(part, ks, arrived)

                return carry

            lax.fori_loop(1, n, each, 0)
        elif event[0] == "att":
            for group in range(groups):
                att_copy(group, False).wait_recv()
        elif event[0] == "project" and fused:
            project(event[1])

    def finish(part, e):
        ks = []
        for d in orders[part]:
            ks.append(e % dims[d][0])
            e = e // dims[d][0]
        return ks

    pair_copy().wait_send()
    for group in range(groups):
        att_copy(group, True).wait_send()
        for level in range(bits):
            @pl.when(sends(level))
            def _():
                state_copy(level, group).wait_send()
    if fused:
        for part in range(len(orders)):
            for e in range(n):
                ks = finish(part, e)
                at, source = source_of(part, ks)
                forward(part, source, at, arrived_by(ks), "wait")
    if not fused:
        stores = [pltpu.make_async_copy(att, att_hbm, load_sem.at[0]), pltpu.make_async_copy(wbuf, w_out_hbm, load_sem.at[1])]
        for store in stores:
            store.start()
        for store in stores:
            store.wait()


def schedule(dims, orders, cuts, n, heads, groups, unrolled):
    bits = n.bit_length() - 1
    whole = sum(size for _, size in cuts)
    timed = []
    for h in range(heads):
        timed.append((0.35 * h / heads, ("within", h)))
    for level in range(bits):
        for group in range(groups):
            timed.append((0.45 + 0.75 * level + 0.25 * group, ("state", level, group)))
    if not unrolled:
        tail = [("loop",), ("att",)]
    else:
        last = {}
        for part, order in enumerate(orders):
            lengths = [dims[d][0] for d in order]
            count = [0] * len(order)
            for rev in itertools.product(*[range(length) for length in lengths[::-1]]):
                ks = rev[::-1]
                arrived = max((r for r, k in enumerate(ks) if k), default=-1)
                if arrived < 0:
                    continue
                count[arrived] += 1
                when = count[arrived] * cuts[part][1] / whole * 1.8 + 0.3 * sum(1 for k in ks if k)
                if arrived == len(order) - 1 and lengths[-1] == 2:
                    when += 100
                timed.append((when, ("weight", part, ks, arrived)))
        tail = [("att",)]
    timed.sort(key=lambda t: t[0])
    return [e for _, e in timed] + tail + [("project", p) for p in range(len(orders))]


def on_device(dims, queries, keys, values, level_pattern, level_weight, out_weight):
    n = lax.axis_size("seq")
    tokens, width = queries.shape
    heads = width // HD
    bits = n.bit_length() - 1
    _, rows, full = out_weight.shape
    cols = full // 2
    fused = rows % 16 == 0
    groups = min(4, heads)
    tiles = cols // 128
    if len(dims) == 3:
        long = max(range(3), key=lambda i: dims[i][0])
        a, b = [i for i in range(3) if i != long]
        orders = [(long, a, b), (long, b, a), (a, b, long)]
        share = max(1, tiles * 3 // 8)
        sizes = [share, share, tiles - 2 * share]
    else:
        orders, sizes = [tuple(range(len(dims)))], [tiles]
    cuts, lo = [], 0
    for size in sizes:
        cuts.append((lo * 128, size * 128))
        lo += size
    events = schedule(dims, orders, cuts, n, heads, groups, fused)
    plan = (dims, orders, cuts, events, n, fused)
    bf16, f32 = jnp.bfloat16, jnp.float32
    any_spec = pl.BlockSpec(memory_space=pl.ANY)
    vmem_spec = pl.BlockSpec(memory_space=pltpu.VMEM)
    if fused:
        out_shape = jax.ShapeDtypeStruct((tokens, cols), f32)
        out_specs = vmem_spec
    else:
        out_shape = [
            jax.ShapeDtypeStruct((2, tokens, width), bf16),
            jax.ShapeDtypeStruct((2, n, rows, cols), bf16),
        ]
        out_specs = [any_spec, any_spec]
    dma = pltpu.SemaphoreType.DMA
    result = pl.pallas_call(
        functools.partial(kernel, plan),
        out_shape=out_shape,
        in_specs=[any_spec] * 3 + [vmem_spec] * 2 + [any_spec],
        out_specs=out_specs,
        scratch_shapes=[
            pltpu.VMEM((tokens, width), bf16),
            pltpu.VMEM((tokens, width), bf16),
            pltpu.VMEM((tokens, width), bf16),
            pltpu.VMEM((1, rows, full), bf16),
            pltpu.VMEM((2, n, rows, cols), bf16),
            pltpu.VMEM((2, tokens, width), bf16),
            pltpu.VMEM((tokens, width), f32),
            pltpu.VMEM((heads, HD, HD), f32),
            pltpu.VMEM((bits, heads, HD, HD), bf16),
            pltpu.VMEM((bits, heads, HD, HD), bf16),
            pltpu.VMEM((bits + 1, tokens, HD), f32),
            dma((4,)),
            dma,
            dma,
            dma,
            dma((len(orders), n if fused else 1, 2 * len(dims))),
            dma((len(orders), n)),
            dma((bits, groups)),
            dma((bits, groups)),
            dma((groups,)),
            dma((groups,)),
        ],
        compiler_params=pltpu.CompilerParams(
            collective_id=0, has_side_effects=True, vmem_limit_bytes=60 * 2**20
        ),
    )(queries, keys, values, level_pattern.reshape(1, tokens), level_weight, out_weight)
    if fused:
        return result
    att, gathered = result
    return jnp.einsum(
        "gtk,gkd->td", att, gathered.reshape(2, n * rows, cols), preferred_element_type=f32
    )


def solution(mesh):
    placed = (
        P("seq", "head"),
        P("seq", "head"),
        P("seq", "head"),
        P("seq"),
        P(),
        P("head", "seq", None),
    )
    return jax.shard_map(
        functools.partial(on_device, line_dims(mesh)),
        mesh=mesh, in_specs=placed, out_specs=P("seq", "head"), check_vma=False,
    )
```

time: 138 us -> 62.4 us (0.45); the launches traced: 136 us -> 62.1 us
  waiting for transfers between devices: 102 us -> 0 us
  Pallas kernels: 0 us -> 58.2 us
  matrix products: 14.9 us -> 0 us
  between operations: 13.5 us -> 0.01 us
  starting transfers between devices: 2.96 us -> 0 us
  local copies, waits for them, and re-layouts: 2.08 us -> 3.97 us
    ppermute x4 -> x0, waiting for transfers between devices: 87.1 us -> none  [swapped(): lax.ppermute(x, axis, [(i, i ^ 1 << stride) for i in range(lax.axis_size(...]
    pallas_call x0 -> x1, Pallas kernels: none -> 58.2 us  [on_device(): pl.pallas_call(functools.partial(kernel, plan), out_shape=out_shape, in_s...]
    dot_general x5 -> x0, matrix products: 14.9 us -> none  [the longest x1 5.73 us: on_device(): jnp.einsum('the,lhef->lthf', query.astype(jnp.float32), jnp.stack(blocks)...]
    reduce_scatter x1 -> x0, waiting for transfers between devices: 13.8 us -> none  [on_device(): lax.psum_scatter(partial_value, 'head', scatter_dimension=1, tiled=True)]
    ppermute x4 -> x0, starting transfers between devices: 2.92 us -> none  [swapped(): lax.ppermute(x, axis, [(i, i ^ 1 << stride) for i in range(lax.axis_size(...]
    unnamed x14 -> x1, local copies, waits for them, and re-layouts: 0.24 us -> 2.73 us
  transfers between devices with their start and end apart: 6 -> 0, of which waited for: 5 -> 0; matrix products, arithmetic and copies ran while one was open for 9% -> 0% of each run, Pallas kernels for 0% -> 0%
where the time goes in v1:
time: 62.4 us; the launch traced here: 62.1 us
  Pallas kernels  58.2 us (93%)
  local copies, waits for them, and re-layouts  3.97 us (6%)
    pallas_call x1, Pallas kernels, on_device(): pl.pallas_call(functools.partial(kernel, plan), out_shape=out_shape, in_s...  58.2 us
    unnamed x1, local copies, waits for them, and re-layouts  2.73 us

profile of v1, /device:TPU:28, one launch (start us, length us, event | category | flops | bytes accessed | tf_op | source)
XLA Modules:
  0.0 62.1 jit_solution(15954531961535745736)
XLA Ops:
  0.0 1.2 %reshape.3.pattern_ref = s32[1,384]{1,0:T(1,128)} reshape(s32[384]{0:T(512)} %param.9) | data formatting | bytes 3072 | tf_op jit(solution)/shard_map/reshape | solution.py:440
  1.2 58.2 %shard_map.64 = f32[384,1024]{1,0:T(8,128)} custom-call(bf16[384,1024]{1,0:T(8,128)(2,1)} %q_hbm.1, bf16[384,1024]{1,0:T(8,128)(2,1)} %k_hbm.1, bf16[384,1024]{1,0:T(8,128)(2,1)} %v_hbm.1, s32[1,384]{1,0:T(1,128)} %reshape.3.pattern_ref, f32[16,9]{1,0:T(8,128)} %table_ref.1, bf16[1,64,2048]{2,1,0:T(8,128)(2,1)} %w_hbm.1), custom_call_target="tpu_custom_call" | custom-call | tf_op jit(solution)/shard_map/pallas_call | solution.py:409
  59.4 2.7 %copy.8 = f32[384,1024]{1,0:T(8,128)} copy(f32[384,1024]{1,0:T(8,128)} %shard_map.64) | data formatting | bytes 3145728

commit v2 on v1

--- a/solution.py
+++ b/solution.py
@@ -51,8 +51,8 @@
         out_ref, *rest = rest
     else:
         att_hbm, w_out_hbm, *rest = rest
-    (q_ref, k_ref, v_ref, w_ref, wbuf, att, acc, sub, outgoing, incoming, mixb,
-     load_sem, own_sem, pair_send, pair_recv, w_send, w_recv, s_send, s_recv, a_send, a_recv) = rest
+    (q_ref, k_ref, v_ref, w_ref, wbuf, att, acc, sub, outgoing, incoming, scale_out, scale_in, mixb,
+     load_sem, own_sem, pair_send, pair_recv, w_send, w_recv, s_send, s_recv, t_send, t_recv, a_send, a_recv) = rest
     me = lax.axis_index("seq")
     core = lax.axis_index("head")
     other = 1 - core
@@ -92,7 +92,7 @@
     for l in range(bits + 1):
         if l == 0:
             ids = lax.broadcasted_iota(jnp.int32, (table_ref.shape[0], tokens), 0)
-            one_hot = (ids == pattern_ref[...]).astype(jnp.float32)
+            one_hot = (ids == pattern_ref[...].reshape(1, tokens)).astype(jnp.float32)
             mix = lax.dot_general(
                 one_hot, table_ref[...], (((0,), (0,)), ((), ())),
                 precision=lax.Precision.HIGHEST, preferred_element_type=jnp.float32,
@@ -106,13 +106,22 @@
     loads[1].wait()
     loads[2].wait()
 
+    def pack_state(level, h, state):
+        top = jnp.maximum(jnp.max(jnp.abs(state), axis=0, keepdims=True), 1e-30)
+        scaled = jnp.round(state * (32767.0 / top))
+        outgoing[level, h] = scaled.astype(jnp.int32).astype(jnp.int16)
+        scale_out[level, h] = jnp.broadcast_to(top * (1.0 / 32767.0), (8, HD))
+
+    def unpack_state(level, h):
+        return incoming[level, h].astype(jnp.int32).astype(jnp.float32) * scale_in[level, h, 0:1]
+
     def make_states(h):
         state = lax.dot_general(
             k_ref[:, head_cols(h)], v_ref[:, head_cols(h)], (((0,), (0,)), ((), ())),
             preferred_element_type=jnp.float32,
         )
         sub[h] = state
-        outgoing[0, h] = state.astype(jnp.bfloat16)
+        pack_state(0, h, state)
 
     for h in range(heads):
         make_states(h)
@@ -147,6 +156,14 @@
             device_id=(me ^ (1 << level), core), device_id_type=MESH,
         )
 
+    def scale_copy(level, group):
+        piece = pl.ds(group * per, per)
+        return pltpu.make_async_remote_copy(
+            src_ref=scale_out.at[level, piece], dst_ref=scale_in.at[level, piece],
+            send_sem=t_send.at[level, group], recv_sem=t_recv.at[level, group],
+            device_id=(me ^ (1 << level), core), device_id_type=MESH,
+        )
+
     def sum_needed(level):
         return me // 2 ** (level + 1) != n // 2 ** (level + 1) - 1
 
@@ -162,6 +179,7 @@
     for group in range(groups):
         @pl.when(sends(0))
         def _():
+            scale_copy(0, group).start()
             state_copy(0, group).start()
 
     def weight_copy(part, source, slot, target):
@@ -208,8 +226,13 @@
             forward(part, source, at, arrived, "wait")
 
     def read_state(level, h):
-        acc[:, head_cols(h)] += mixb[level + 1] * jnp.dot(
-            q_ref[:, head_cols(h)], incoming[level, h], preferred_element_type=jnp.float32
+        block = unpack_state(level, h)
+        high = block.astype(jnp.bfloat16)
+        low = (block - high.astype(jnp.float32)).astype(jnp.bfloat16)
+        query = q_ref[:, head_cols(h)]
+        acc[:, head_cols(h)] += mixb[level + 1] * (
+            jnp.dot(query, high, preferred_element_type=jnp.float32)
+            + jnp.dot(query, low, preferred_element_type=jnp.float32)
         )
 
     def within_event(h):
@@ -235,6 +258,7 @@
     def state_event(level, group):
         @pl.when(receives(level))
         def _():
+            scale_copy(level, group).wait_recv()
             state_copy(level, group).wait_recv()
 
         span = range(group * per, (group + 1) * per)
@@ -242,12 +266,13 @@
             @pl.when(sum_needed(level))
             def _():
                 for h in span:
-                    summed = sub[h] + incoming[level, h].astype(jnp.float32)
+                    summed = sub[h] + unpack_state(level, h)
                     sub[h] = summed
-                    outgoing[level + 1, h] = summed.astype(jnp.bfloat16)
+                    pack_state(level + 1, h, summed)
 
             @pl.when(sends(level + 1))
             def _():
+                scale_copy(level + 1, group).start()
                 state_copy(level + 1, group).start()
 
         @pl.when(active(level))
@@ -323,6 +348,7 @@
         for level in range(bits):
             @pl.when(sends(level))
             def _():
+                scale_copy(level, group).wait_send()
                 state_copy(level, group).wait_send()
     if fused:
         for part in range(len(orders)):
@@ -420,8 +446,10 @@
             pltpu.VMEM((2, tokens, width), bf16),
             pltpu.VMEM((tokens, width), f32),
             pltpu.VMEM((heads, HD, HD), f32),
-            pltpu.VMEM((bits, heads, HD, HD), bf16),
-            pltpu.VMEM((bits, heads, HD, HD), bf16),
+            pltpu.VMEM((bits, heads, HD, HD), jnp.int16),
+            pltpu.VMEM((bits, heads, HD, HD), jnp.int16),
+            pltpu.VMEM((bits, heads, 8, HD), f32),
+            pltpu.VMEM((bits, heads, 8, HD), f32),
             pltpu.VMEM((bits + 1, tokens, HD), f32),
             dma((4,)),
             dma,
@@ -431,13 +459,15 @@
             dma((len(orders), n)),
             dma((bits, groups)),
             dma((bits, groups)),
+            dma((bits, groups)),
+            dma((bits, groups)),
             dma((groups,)),
             dma((groups,)),
         ],
         compiler_params=pltpu.CompilerParams(
             collective_id=0, has_side_effects=True, vmem_limit_bytes=60 * 2**20
         ),
-    )(queries, keys, values, level_pattern.reshape(1, tokens), level_weight, out_weight)
+    )(queries, keys, values, level_pattern, level_weight, out_weight)
     if fused:
         return result
     att, gathered = result

time: 62.4 us -> 63 us (level)
  Pallas kernels: 58.2 us -> 60 us
  local copies, waits for them, and re-layouts: 3.97 us -> 2.73 us
    pallas_call x1, Pallas kernels: 58.2 us -> 60 us  [on_device(): pl.pallas_call(functools.partial(kernel, plan), out_shape=out_shape, in_s...]
    reshape x1 -> x0, local copies, waits for them, and re-layouts: 1.24 us -> none  [on_device(): level_pattern.reshape(1, tokens)]
where the time goes in v2:
time: 63 us; the launch traced here: 62.8 us
  Pallas kernels  60 us (95%)
  local copies, waits for them, and re-layouts  2.73 us (4%)
    pallas_call x1, Pallas kernels, on_device(): pl.pallas_call(functools.partial(kernel, plan), out_shape=out_shape, in_s...  60 us
    unnamed x1, local copies, waits for them, and re-layouts  2.73 us

profile of v2, /device:TPU:28, one launch (start us, length us, event | category | flops | bytes accessed | tf_op | source)
XLA Modules:
  0.0 62.8 jit_solution(11051430214926238528)
XLA Ops:
  0.0 60.0 %shard_map.64 = f32[384,1024]{1,0:T(8,128)} custom-call(bf16[384,1024]{1,0:T(8,128)(2,1)} %q_hbm.1, bf16[384,1024]{1,0:T(8,128)(2,1)} %k_hbm.1, bf16[384,1024]{1,0:T(8,128)(2,1)} %v_hbm.1, s32[384]{0:T(512)} %pattern_ref.1, f32[16,9]{1,0:T(8,128)} %table_ref.1, bf16[1,64,2048]{2,1,0:T(8,128)(2,1)} %w_hbm.1), custom_call_target="tpu_custom_call" | custom-call | tf_op jit(solution)/shard_map/pallas_call | solution.py:435
  60.0 2.7 %copy.8 = f32[384,1024]{1,0:T(8,128)} copy(f32[384,1024]{1,0:T(8,128)} %shard_map.64) | data formatting | bytes 3145728

commit v3 on v2

--- a/solution.py
+++ b/solution.py
@@ -52,7 +52,7 @@
     else:
         att_hbm, w_out_hbm, *rest = rest
     (q_ref, k_ref, v_ref, w_ref, wbuf, att, acc, sub, outgoing, incoming, scale_out, scale_in, mixb,
-     load_sem, own_sem, pair_send, pair_recv, w_send, w_recv, s_send, s_recv, t_send, t_recv, a_send, a_recv) = rest
+     load_sem, own_sem, pair_send, pair_recv, w_send, w_recv, s_send, s_recv, t_send, t_recv, a_send, a_recv, out_v, out_sem) = rest
     me = lax.axis_index("seq")
     core = lax.axis_index("head")
     other = 1 - core
@@ -298,9 +298,13 @@
         lo, size = cuts[part]
         columns = slice(lo, lo + size)
         flat = [wbuf[g, :, :, columns].reshape(-1, size) for g in range(2)]
-        out_ref[:, columns] = jnp.dot(att[0], flat[0], preferred_element_type=jnp.float32) + jnp.dot(
+        out_v[:, columns] = jnp.dot(att[0], flat[0], preferred_element_type=jnp.float32) + jnp.dot(
             att[1], flat[1], preferred_element_type=jnp.float32
         )
+
+    def out_copy(part):
+        columns = pl.ds(*cuts[part])
+        return pltpu.make_async_copy(out_v.at[:, columns], out_ref.at[:, columns], out_sem.at[part])
 
     for event in events:
         if event[0] == "within":
@@ -334,6 +338,7 @@
                 att_copy(group, False).wait_recv()
         elif event[0] == "project" and fused:
             project(event[1])
+            out_copy(event[1]).start()
 
     def finish(part, e):
         ks = []
@@ -356,7 +361,10 @@
                 ks = finish(part, e)
                 at, source = source_of(part, ks)
                 forward(part, source, at, arrived_by(ks), "wait")
-    if not fused:
+    if fused:
+        for part in range(len(orders)):
+            out_copy(part).wait()
+    else:
         stores = [pltpu.make_async_copy(att, att_hbm, load_sem.at[0]), pltpu.make_async_copy(wbuf, w_out_hbm, load_sem.at[1])]
         for store in stores:
             store.start()
@@ -424,7 +432,7 @@
     vmem_spec = pl.BlockSpec(memory_space=pltpu.VMEM)
     if fused:
         out_shape = jax.ShapeDtypeStruct((tokens, cols), f32)
-        out_specs = vmem_spec
+        out_specs = any_spec
     else:
         out_shape = [
             jax.ShapeDtypeStruct((2, tokens, width), bf16),
@@ -463,6 +471,8 @@
             dma((bits, groups)),
             dma((groups,)),
             dma((groups,)),
+            pltpu.VMEM((tokens, cols) if fused else (8, 128), f32),
+            dma((len(orders),)),
         ],
         compiler_params=pltpu.CompilerParams(
             collective_id=0, has_side_effects=True, vmem_limit_bytes=60 * 2**20

time: 63 us -> 62.7 us (level)
  no operation moved by 1% of the time
where the time goes in v3:
time: 62.7 us; the launch traced here: 62.5 us
  Pallas kernels  59.8 us (95%)
  local copies, waits for them, and re-layouts  2.73 us (4%)
    pallas_call x1, Pallas kernels, on_device(): pl.pallas_call(functools.partial(kernel, plan), out_shape=out_shape, in_s...  59.8 us
    unnamed x1, local copies, waits for them, and re-layouts  2.73 us

profile of v3, /device:TPU:28, one launch (start us, length us, event | category | flops | bytes accessed | tf_op | source)
XLA Modules:
  0.0 62.5 jit_solution(9577965482058530529)
XLA Ops:
  0.0 59.8 %shard_map.64 = f32[384,1024]{1,0:T(8,128)} custom-call(bf16[384,1024]{1,0:T(8,128)(2,1)} %q_hbm.1, bf16[384,1024]{1,0:T(8,128)(2,1)} %k_hbm.1, bf16[384,1024]{1,0:T(8,128)(2,1)} %v_hbm.1, s32[384]{0:T(512)} %pattern_ref.1, f32[16,9]{1,0:T(8,128)} %table_ref.1, bf16[1,64,2048]{2,1,0:T(8,128)(2,1)} %w_hbm.1), custom_call_target="tpu_custom_call" | custom-call | tf_op jit(solution)/shard_map/pallas_call | solution.py:443
  59.8 2.7 %copy.8 = f32[384,1024]{1,0:T(8,128)} copy(f32[384,1024]{1,0:T(8,128)} %shard_map.64) | data formatting | bytes 3145728
